TPU v7x, 512 devices: a whole 4x8x8 slice. The times are simulated.
512 devices in a mesh: img: 8 (over y_lo, core), fsdp: 64 (over x, z, y_hi).
Axes of the slice: x: 4, y: 8 (y_hi: 2, y_lo: 4; y = y_hi * 4 + y_lo), z: 8, core: 2. Of those that a mesh axis runs over, the one named last changes fastest.
Arguments:
- text_states: bfloat16 [16384, 8192], P('fsdp')
- text_gain: float32 [8192], replicated, may hold values from 0.1 to 1.9
- vision: bfloat16 [8, 512, 8192], P('img', 'fsdp'), may hold values from -6 to 6
- q_weight: bfloat16 [8192, 4096], P('fsdp', 'img'), may hold values from -0.0625 to 0.0625
- k_weight: bfloat16 [8192, 1024], P('fsdp', 'img'), may hold values from -0.0625 to 0.0625
- v_weight: bfloat16 [8192, 1024], P('fsdp', 'img'), may hold values from -0.0625 to 0.0625
- q_gain: float32 [128], replicated, may hold values from 1 to 16
- k_gain: float32 [128], replicated, may hold values from 1 to 16
- owners: int32 [256, 4], P('fsdp'), may hold values from 0 to 7
- counts: int32 [256], P('fsdp'), may hold values from 0 to 4
- gate_value: float32 [1], replicated, may hold values from 0.3 to 1.5
Outputs:
- attended: bfloat16 [16384, 4096], P('fsdp', 'img')
All inputs are finite; a program needn't handle non-finite values.
Results may differ from a plain program's by a relative error of at most 0.025.
The roundings to bfloat16 on the way count: a program that leaves them out, or rounds other values in their place, can miss the bound.
Values may be sent and summed in bfloat16 or wider, within the bound.
No kernel may reach another device: no remote copies, remote signals or barrier semaphores. Data moves between devices by JAX's collectives and lax.ppermute only.
A program may use at most 64 MiB of HBM per device.

v0:
```python
import jax
import jax.numpy as jnp
from jax import lax
from jax.sharding import PartitionSpec as P

norm_epsilon = 1e-05
masked_score = -1e30


def head_norm(values, gain):
    mean_square = jnp.mean(values * values, axis=-1, keepdims=True)
    return values * lax.rsqrt(mean_square + norm_epsilon) * gain


def on_device(
    text_states,
    text_gain,
    vision,
    q_weight,
    k_weight,
    v_weight,
    q_gain,
    k_gain,
    owners,
    counts,
    gate_value,
):
    token_rows = text_states.shape[0]
    width = text_states.shape[1]
    head_size = q_gain.shape[0]
    per_group = q_weight.shape[1] // head_size
    images = lax.axis_size("img")
    shard_tokens = vision.shape[1]
    text_float = text_states.astype(jnp.float32)
    normed = (
        text_float
        * lax.rsqrt(jnp.mean(text_float * text_float, axis=-1, keepdims=True) + norm_epsilon)
        * text_gain
    ).astype(jnp.bfloat16)
    visual = lax.all_gather(vision, "img", axis=0, tiled=True).reshape(images * shard_tokens, width)
    columns = visual
    joined = jnp.concatenate(
        (
            lax.all_gather(k_weight, "fsdp", axis=0, tiled=True),
            lax.all_gather(v_weight, "fsdp", axis=0, tiled=True),
        ),
        axis=1,
    )
    pair_full = jnp.dot(columns, joined, preferred_element_type=jnp.float32)
    columns = normed
    query_full = jnp.dot(
        columns,
        lax.all_gather(q_weight, "fsdp", axis=0, tiled=True),
        preferred_element_type=jnp.float32,
    )
    row_count = token_rows * per_group
    queries = (
        head_norm(query_full.reshape(token_rows, per_group, head_size), q_gain)
        .astype(jnp.bfloat16)
        .reshape(row_count, head_size)
    )
    keys = (
        head_norm(pair_full[:, :head_size], k_gain)
        .astype(jnp.bfloat16)
        .reshape(images, shard_tokens, head_size)
    )
    values = pair_full[:, head_size:].astype(jnp.bfloat16).reshape(images, shard_tokens, head_size)
    block_count = owners.shape[0]
    live_slot = jnp.arange(owners.shape[1], dtype=jnp.int32)[None, :] < counts[:, None]
    matched = (
        owners[:, :, None] == jnp.arange(images, dtype=jnp.int32)[None, None, :]
    ) & live_slot[:, :, None]
    block_images = jnp.any(matched, axis=1)
    token_images = jnp.broadcast_to(
        block_images[:, None, :], (block_count, token_rows // block_count, images)
    ).reshape(token_rows, images)
    row_live = jnp.any(token_images, axis=1)
    score_scale = head_size ** (-0.5)
    key_piece = lax.all_gather(keys, "fsdp", axis=1, tiled=True)
    value_piece = lax.all_gather(values, "fsdp", axis=1, tiled=True)
    key_count = key_piece.shape[1]
    allowed = jnp.broadcast_to(token_images[:, :, None], (token_rows, images, key_count)).reshape(
        token_rows, images * key_count
    )
    running_max = jnp.full((row_count,), masked_score, jnp.float32)
    scores = (
        jnp.einsum(
            "rd,kd->rk",
            queries,
            key_piece.reshape(images * key_count, head_size),
            preferred_element_type=jnp.float32,
        )
        * score_scale
    )
    scores = jnp.where(
        allowed[:, None, :], scores.reshape(token_rows, per_group, -1), masked_score
    ).reshape(row_count, -1)
    new_max = jnp.maximum(running_max, jnp.max(scores, axis=1))
    weights = jnp.exp(scores - new_max[:, None]).astype(jnp.bfloat16)
    denominator = jnp.sum(weights.astype(jnp.float32), axis=1)
    numerator = jnp.dot(
        weights,
        value_piece.reshape(images * key_count, head_size),
        preferred_element_type=jnp.float32,
    )
    running_max, denominator, numerator = (new_max, denominator, numerator)
    live_rows = jnp.broadcast_to(row_live[:, None], (token_rows, per_group)).reshape(row_count)
    safe_denominator = jnp.where(live_rows, denominator, jnp.float32(1.0))
    factor = jnp.where(live_rows, jnp.tanh(gate_value[0]), jnp.float32(0.0))
    attended = numerator / safe_denominator[:, None] * factor[:, None]
    return attended.reshape(token_rows, per_group * head_size).astype(jnp.bfloat16)


def solution(mesh):
    in_specs = (
        P("fsdp", None),
        P(),
        P("img", "fsdp", None),
        P("fsdp", "img"),
        P("fsdp", "img"),
        P("fsdp", "img"),
        P(),
        P(),
        P("fsdp", None),
        P("fsdp"),
        P(),
    )
    out_specs = P("fsdp", "img")
    return jax.shard_map(
        on_device, mesh=mesh, in_specs=in_specs, out_specs=out_specs, check_vma=False
    )
```

profile of v0, /device:TPU:22, one launch (start us, length us, event | category | flops | bytes accessed | tf_op | source)
XLA Modules:
  0.0 737.3 jit_solution(17077881853206447943)
XLA Ops:
  6.5 0.0 copy-start
  6.5 0.0 all-gather.13.cloned.1.call-start
  6.5 0.7 all-gather.13.cloned.1.call-update
  7.3 0.0 all-gather.11.cloned.1.call-start
  7.3 0.7 all-gather.11.cloned.1.call-update
  8.0 0.0 all-gather.9.cloned.1.call-start
  8.1 0.7 all-gather.9.cloned.1.call-update
  8.7 0.0 all-gather.7.cloned.1.call-start
  8.8 0.5 all-gather.7.cloned.1.call-update
  9.3 0.0 all-gather.15.cloned.1.call-start
  9.4 38.2 %all-gather.13.cloned.1.call-done = bf16[8,8,8192]{2,1,0:T(8,128)(2,1)} async-done(((bf16[1,8,8192]{2,1,0:T(8,128)(2,1)}), bf16[8,8,8192]{2,1,0:T(8,128)(2,1)}) %all-gather.13.cloned.1.call-update) | async-done | bytes 1048592 | tf_op jit(solution)/shard_map/all_gather | solution.py:40
  47.6 143.9 %all-gather.11.cloned.1.call-done = bf16[8192,128]{1,0:T(8,128)(2,1)} async-done(((bf16[128,128]{1,0:T(8,128)(2,1)}), bf16[8192,128]{1,0:T(8,128)(2,1)}) %all-gather.11.cloned.1.call-update) | async-done | bytes 2097168 | tf_op jit(solution)/shard_map/all_gather | solution.py:45
  191.5 134.0 %all-gather.9.cloned.1.call-done = bf16[8192,128]{1,0:T(8,128)(2,1)} async-done(((bf16[128,128]{1,0:T(8,128)(2,1)}), bf16[8192,128]{1,0:T(8,128)(2,1)}) %all-gather.9.cloned.1.call-update) | async-done | bytes 2097168 | tf_op jit(solution)/shard_map/all_gather | solution.py:44
  325.5 3.3 fusion.14
  328.9 0.1 multiply_reduce_fusion
  329.0 1.3 fusion.20
  330.4 0.0 all-gather.15.cloned.1.call-update
  330.4 0.0 all-gather.17.cloned.1.call-start
  330.4 0.7 iota_compare_fusion.1
  331.2 0.9 fusion.23
  332.1 0.5 broadcast_in_dim.68
  332.6 0.8 copy.15
  333.3 0.0 copy-start.2
  333.3 5.7 broadcast_in_dim.70
  339.0 12.4 %broadcast_in_dim.71 = pred[1024,4096]{1,0:T(32,128)(4,1)} reshape(pred[256,4,4096]{2,1,0:T(4,128)(4,1)} %broadcast_in_dim.70) | data formatting | bytes 8388608 | tf_op jit(solution)/shard_map/jit(_where)/broadcast_in_dim | solution.py:95
  351.4 0.1 reduce_or.22
  351.5 0.1 broadcast_in_dim.74
  351.5 0.1 broadcast_in_dim.75
  351.7 0.1 reshape.111
  352.5 3.1 fusion.1
  355.6 0.0 copy-done
  355.6 0.6 fusion.21
  356.2 0.0 all-gather.17.cloned.1.call-update
  356.3 156.7 %all-gather.7.cloned.1.call-done = bf16[8192,512]{1,0:T(8,128)(2,1)} async-done(((bf16[128,512]{1,0:T(8,128)(2,1)}), bf16[8192,512]{1,0:T(8,128)(2,1)}) %all-gather.7.cloned.1.call-update) | async-done | bytes 8388624 | tf_op jit(solution)/shard_map/all_gather | solution.py:53
  513.0 0.0 copy-done.2
  513.0 7.0 fusion.26
  520.0 0.2 mul.90
  520.2 0.3 reduce_sum.37
  520.6 0.3 mul.91
  520.9 0.1 fusion.19
  521.0 0.2 convert_element_type.32
  521.2 95.6 %all-gather.15.cloned.1.call-done = bf16[8,512,128]{2,1,0:T(8,128)(2,1)} async-done(((bf16[8,8,128]{2,1,0:T(8,128)(2,1)}), bf16[8,512,128]{2,1,0:T(8,128)(2,1)}) %all-gather.15.cloned.1.call-update) | async-done | bytes 1048592 | tf_op jit(solution)/shard_map/all_gather | solution.py:79
  616.8 6.0 fusion
  622.8 0.0 copy-done.1
  622.8 7.4 %convert_reduce_fusion = (f32[1024]{0:T(1024)S(1)}, bf16[1024,4096]{1,0:T(8,128)(2,1)}) fusion(f32[1024]{0:T(1024)S(1)} %broadcast_maximum_fusion, pred[1024,4096]{1,0:T(32,128)(4,1)S(1)} %copy-done.1, f32[1024,4096]{1,0:T(8,128)S(1)} %get-tuple-element.14), kind=kLoop, calls=%fused_computation | loop fusion | flops 25164800 | bytes 29368320 | tf_op jit(solution)/shard_map/reduce_sum | solution.py:100
  630.3 93.4 %all-gather.17.cloned.1.call-done = bf16[8,512,128]{2,1,0:T(8,128)(2,1)} async-done(((bf16[8,8,128]{2,1,0:T(8,128)(2,1)}), bf16[8,512,128]{2,1,0:T(8,128)(2,1)}) %all-gather.17.cloned.1.call-update) | async-done | bytes 1048592 | tf_op jit(solution)/shard_map/all_gather | solution.py:80
  723.7 5.9 fusion.13
  729.6 0.9 convert_element_type.37
  (8 shorter events, 0.1 us)
Async XLA Ops:
  6.5 349.1 %copy-start = (f32[128]{0:T(128)S(1)}, f32[128]{0:T(128)}, u32[]{:S(2)}) copy-start(f32[128]{0:T(128)} %param.17) | copy-start | bytes 1540
  6.5 41.0 %all-gather.13.cloned.1.call-start = ((), (), s32[]{:S(2)}) async-start(), calls=%async_computation.3 | async-start | bytes 1179648 | tf_op jit(solution)/shard_map/all_gather | solution.py:40
  7.3 184.2 %all-gather.11.cloned.1.call-start = ((), (), s32[]{:S(2)}) async-start(), calls=%async_computation.2 | async-start | bytes 2129920 | tf_op jit(solution)/shard_map/all_gather | solution.py:45
  8.0 317.5 %all-gather.9.cloned.1.call-start = ((), (), s32[]{:S(2)}) async-start(), calls=%async_computation.1 | async-start | bytes 2129920 | tf_op jit(solution)/shard_map/all_gather | solution.py:44
  8.7 504.2 %all-gather.7.cloned.1.call-start = ((), (), s32[]{:S(2)}) async-start(), calls=%async_computation | async-start | bytes 8519680 | tf_op jit(solution)/shard_map/all_gather | solution.py:53
  9.3 607.5 %all-gather.15.cloned.1.call-start = ((), (), s32[]{:S(2)}) async-start(), calls=%async_computation.4 | async-start | bytes 1064960 | tf_op jit(solution)/shard_map/all_gather | solution.py:79
  330.4 393.3 %all-gather.17.cloned.1.call-start = ((), (), s32[]{:S(2)}) async-start(), calls=%async_computation.5 | async-start | bytes 1064960 | tf_op jit(solution)/shard_map/all_gather | solution.py:80
  333.3 179.6 %copy-start.2 = (f32[8192]{0:T(1024)S(1)}, f32[8192]{0:T(1024)}, u32[]{:S(2)}) copy-start(f32[8192]{0:T(1024)} %param.12) | copy-start | bytes 98308
  616.8 6.0 copy-start.1
Sparse Core Ops, SparseCore 0:
  9.4 38.1 all-gather.12
  52.0 139.4 all-gather.10
  196.0 129.5 all-gather.8
  329.9 183.0 all-gather.6
  517.1 99.6 all-gather.14
  621.0 102.6 all-gather.16
where the time goes:
time: 738 us; the launch traced here: 737 us
  waiting for transfers between devices  665 us (90%)
  matrix products  22.3 us (3%)
  local copies, waits for them, and re-layouts  21.8 us (3%)
  between operations  14.3 us (2%)
  other arithmetic  14.1 us (2%)
    all_gather x1, waiting for transfers between devices, on_device(): lax.all_gather(q_weight, 'fsdp', axis=0, tiled=True)  157 us
    all_gather x1, waiting for transfers between devices, on_device(): lax.all_gather(v_weight, 'fsdp', axis=0, tiled=True)  144 us
    all_gather x1, waiting for transfers between devices, on_device(): lax.all_gather(k_weight, 'fsdp', axis=0, tiled=True)  134 us
    all_gather x1, waiting for transfers between devices, on_device(): key_piece = lax.all_gather(keys, 'fsdp', axis=1, tiled=True)  95.6 us
    all_gather x1, waiting for transfers between devices, on_device(): value_piece = lax.all_gather(values, 'fsdp', axis=1, tiled=True)  93.4 us
    all_gather x1, waiting for transfers between devices, on_device(): lax.all_gather(vision, 'img', axis=0, tiled=True)  38.2 us
    broadcast_in_dim x2, local copies, waits for them, and re-layouts, on_device(): jnp.where(allowed[:, None, :], scores.reshape(token_rows, per_group, -1),...  18 us
  transfers between devices with their start and end apart: 6, of which 6 were waited for; matrix products, arithmetic and copies ran while one was open for 7% of the time, Pallas kernels for 0%

commit v1 on v0

--- a/solution.py
+++ b/solution.py
@@ -77,7 +77,10 @@
     row_live = jnp.any(token_images, axis=1)
     score_scale = head_size ** (-0.5)
     key_piece = lax.all_gather(keys, "fsdp", axis=1, tiled=True)
-    value_piece = lax.all_gather(values, "fsdp", axis=1, tiled=True)
+    size = lax.axis_size("fsdp")
+    blocks = jnp.stack([values for _ in range(size)])
+    blocks = lax.all_to_all(blocks, "fsdp", split_axis=0, concat_axis=0)
+    value_piece = jnp.concatenate(blocks, axis=1)
     key_count = key_piece.shape[1]
     allowed = jnp.broadcast_to(token_images[:, :, None], (token_rows, images, key_count)).reshape(
         token_rows, images * key_count

time: 738 us -> 652 us (0.88)
  waiting for transfers between devices: 665 us -> 576 us
  starting transfers between devices: 0.2 us -> 9.81 us
    all_gather x1 -> x0, waiting for transfers between devices: 93.4 us -> none  [on_device(): value_piece = lax.all_gather(values, 'fsdp', axis=1, tiled=True)]
    all_to_all x0 -> x1, starting transfers between devices: none -> 9.62 us  [on_device(): blocks = lax.all_to_all(blocks, 'fsdp', split_axis=0, concat_axis=0)]
  transfers between devices with their start and end apart: 6 -> 6, of which waited for: 6 -> 6; matrix products, arithmetic and copies ran while one was open for 7% -> 6% of each run, Pallas kernels for 0% -> 0%
where the time goes in v1:
time: 652 us
  waiting for transfers between devices  576 us (88%)
  local copies, waits for them, and re-layouts  22.7 us (3%)
  matrix products  18.5 us (3%)
  between operations  14.1 us (2%)
  other arithmetic  10.8 us (2%)
  starting transfers between devices  9.81 us (2%)
    all_gather x1, waiting for transfers between devices, on_device(): lax.all_gather(q_weight, 'fsdp', axis=0, tiled=True)  159 us
    all_gather x1, waiting for transfers between devices, on_device(): lax.all_gather(v_weight, 'fsdp', axis=0, tiled=True)  144 us
    all_gather x1, waiting for transfers between devices, on_device(): lax.all_gather(k_weight, 'fsdp', axis=0, tiled=True)  134 us
    all_gather x1, waiting for transfers between devices, on_device(): key_piece = lax.all_gather(keys, 'fsdp', axis=1, tiled=True)  95.6 us
    all_gather x1, waiting for transfers between devices, on_device(): lax.all_gather(vision, 'img', axis=0, tiled=True)  38.3 us
    broadcast_in_dim x2, local copies, waits for them, and re-layouts, on_device(): jnp.where(allowed[:, None, :], scores.reshape(token_rows, per_group, -1),...  18.1 us
  transfers between devices with their start and end apart: 6, of which 6 were waited for; matrix products, arithmetic and copies ran while one was open for 6% of the time, Pallas kernels for 0%

profile of v1, /device:TPU:22, one launch (start us, length us, event | category | flops | bytes accessed | tf_op | source)
XLA Modules:
  0.0 651.6 jit_solution(10841167907279179230)
XLA Ops:
  6.5 0.0 copy-start
  6.5 0.0 all-gather.12.cloned.1.call-start
  6.6 0.7 all-gather.12.cloned.1.call-update
  7.3 0.0 all-gather.10.cloned.1.call-start
  7.3 0.7 all-gather.10.cloned.1.call-update
  8.0 0.0 all-gather.8.cloned.1.call-start
  8.1 0.7 all-gather.8.cloned.1.call-update
  8.8 0.0 all-gather.6.cloned.1.call-start
  8.8 0.5 all-gather.6.cloned.1.call-update
  9.3 38.3 %all-gather.12.cloned.1.call-done = bf16[8,8,8192]{2,1,0:T(8,128)(2,1)} async-done(((bf16[1,8,8192]{2,1,0:T(8,128)(2,1)}), bf16[8,8,8192]{2,1,0:T(8,128)(2,1)}) %all-gather.12.cloned.1.call-update) | async-done | bytes 1048592 | tf_op jit(solution)/shard_map/all_gather | solution.py:40
  47.6 143.9 %all-gather.10.cloned.1.call-done = bf16[8192,128]{1,0:T(8,128)(2,1)} async-done(((bf16[128,128]{1,0:T(8,128)(2,1)}), bf16[8192,128]{1,0:T(8,128)(2,1)}) %all-gather.10.cloned.1.call-update) | async-done | bytes 2097168 | tf_op jit(solution)/shard_map/all_gather | solution.py:45
  191.5 134.0 %all-gather.8.cloned.1.call-done = bf16[8192,128]{1,0:T(8,128)(2,1)} async-done(((bf16[128,128]{1,0:T(8,128)(2,1)}), bf16[8192,128]{1,0:T(8,128)(2,1)}) %all-gather.8.cloned.1.call-update) | async-done | bytes 2097168 | tf_op jit(solution)/shard_map/all_gather | solution.py:44
  325.6 3.3 fusion.14
  328.9 1.3 stack.3
  330.2 9.6 %all-to-all-start = ((bf16[64,8,8,128]{3,2,1,0:T(8,128)(2,1)}), bf16[64,8,8,128]{3,2,1,0:T(8,128)(2,1)S(1)}, u32[]{:S(2)}, u32[]{:S(2)}) async-start(bf16[64,8,8,128]{3,2,1,0:T(8,128)(2,1)} %stack.3), calls=%async_computation | async-start | bytes 2097152 | tf_op jit(solution)/shard_map/all_to_all | solution.py:82
  339.8 0.0 all-gather.14.cloned.1.call-start
  339.9 3.2 fusion.1
  343.1 0.1 multiply_reduce_fusion
  343.2 0.0 copy-done.3
  343.2 0.7 fusion.20
  343.9 0.0 all-gather.14.cloned.1.call-update
  343.9 0.0 copy-done.5
  343.9 0.1 iota_compare_fusion.1
  344.0 0.0 copy-done.2
  344.0 0.2 fusion.23
  344.2 0.5 broadcast_in_dim.68
  344.7 0.8 copy.19
  345.5 0.0 copy-start.4
  345.5 5.7 broadcast_in_dim.70
  351.2 12.4 %broadcast_in_dim.71 = pred[1024,4096]{1,0:T(32,128)(4,1)} reshape(pred[256,4,4096]{2,1,0:T(4,128)(4,1)} %broadcast_in_dim.70) | data formatting | bytes 8388608 | tf_op jit(solution)/shard_map/jit(_where)/broadcast_in_dim | solution.py:98
  363.5 0.1 reduce_or.22
  363.6 0.1 broadcast_in_dim.74
  363.7 0.1 broadcast_in_dim.75
  363.8 0.1 reshape.109
  364.7 2.2 all-to-all-done
  366.9 0.2 copy.18
  367.1 159.0 %all-gather.6.cloned.1.call-done = bf16[8192,512]{1,0:T(8,128)(2,1)} async-done(((bf16[128,512]{1,0:T(8,128)(2,1)}), bf16[8192,512]{1,0:T(8,128)(2,1)}) %all-gather.6.cloned.1.call-update) | async-done | bytes 8388624 | tf_op jit(solution)/shard_map/all_gather | solution.py:53
  526.1 7.0 %fusion.26 = (f32[256,512]{1,0:T(8,128)S(1)}, f32[256,512]{1,0:T(8,128)S(1)}) fusion(bf16[8192,512]{1,0:T(8,128)(2,1)} %all-gather.6.cloned.1.call-done, bf16[256,8192]{1,0:T(8,128)(2,1)} %param.11, f32[8192]{0:T(1024)S(1)} %copy-done.4, f32[256]{0:T(256)S(1)} %add_rsqrt_fusion.1), kind=kOutput, calls=%fused_computation.42 | convolution fusion | flops 2156003328 | bytes 13665280 | tf_op jit(solution)/shard_map/dot_general | solution.py:51
  533.1 0.2 mul.90
  533.3 0.3 reduce_sum.37
  533.7 0.3 mul.91
  534.0 0.1 fusion.19
  534.2 0.2 convert_element_type.32
  534.3 95.6 %all-gather.14.cloned.1.call-done = bf16[8,512,128]{2,1,0:T(8,128)(2,1)} async-done(((bf16[8,8,128]{2,1,0:T(8,128)(2,1)}), bf16[8,512,128]{2,1,0:T(8,128)(2,1)}) %all-gather.14.cloned.1.call-update) | async-done | bytes 1048592 | tf_op jit(solution)/shard_map/all_gather | solution.py:79
  629.9 5.8 fusion
  635.8 6.1 convert_reduce_fusion
  641.8 2.3 fusion.13
  644.2 0.9 convert_element_type.37
  (15 shorter events, 0.1 us)
Async XLA Ops:
  6.5 358.1 %copy-start = (f32[128]{0:T(128)S(1)}, f32[128]{0:T(128)}, u32[]{:S(2)}) copy-start(f32[128]{0:T(128)} %param.17) | copy-start | bytes 1540
  6.5 336.6 %copy-start.3 = (f32[128]{0:T(128)S(1)}, f32[128]{0:T(128)}, u32[]{:S(2)}) copy-start(f32[128]{0:T(128)} %param.18) | copy-start | bytes 1540
  6.5 337.4 %copy-start.5 = (s32[4]{0:T(128)S(1)}, s32[4]{0:T(128)}, u32[]{:S(2)}) copy-start(s32[4]{0:T(128)} %param.20) | copy-start | bytes 52
  6.5 337.4 %copy-start.2 = (s32[4,4]{1,0:T(4,128)S(1)}, s32[4,4]{1,0:T(4,128)}, u32[]{:S(2)}) copy-start(s32[4,4]{1,0:T(4,128)} %param.19) | copy-start | bytes 196
  6.5 41.1 %all-gather.12.cloned.1.call-start = ((), (), s32[]{:S(2)}) async-start(), calls=%async_computation.4 | async-start | bytes 1179648 | tf_op jit(solution)/shard_map/all_gather | solution.py:40
  7.3 184.2 %all-gather.10.cloned.1.call-start = ((), (), s32[]{:S(2)}) async-start(), calls=%async_computation.3 | async-start | bytes 2129920 | tf_op jit(solution)/shard_map/all_gather | solution.py:45
  8.0 317.5 %all-gather.8.cloned.1.call-start = ((), (), s32[]{:S(2)}) async-start(), calls=%async_computation.2 | async-start | bytes 2129920 | tf_op jit(solution)/shard_map/all_gather | solution.py:44
  8.8 517.3 %all-gather.6.cloned.1.call-start = ((), (), s32[]{:S(2)}) async-start(), calls=%async_computation.1 | async-start | bytes 8519680 | tf_op jit(solution)/shard_map/all_gather | solution.py:53
  330.2 36.7 %all-to-all-start = ((bf16[64,8,8,128]{3,2,1,0:T(8,128)(2,1)}), bf16[64,8,8,128]{3,2,1,0:T(8,128)(2,1)S(1)}, u32[]{:S(2)}, u32[]{:S(2)}) async-start(bf16[64,8,8,128]{3,2,1,0:T(8,128)(2,1)} %stack.3), calls=%async_computation | async-start | bytes 2097152 | tf_op jit(solution)/shard_map/all_to_all | solution.py:82
  339.8 290.1 %all-gather.14.cloned.1.call-start = ((), (), s32[]{:S(2)}) async-start(), calls=%async_computation.5 | async-start | bytes 1064960 | tf_op jit(solution)/shard_map/all_gather | solution.py:79
  345.5 180.6 %copy-start.4 = (f32[8192]{0:T(1024)S(1)}, f32[8192]{0:T(1024)}, u32[]{:S(2)}) copy-start(f32[8192]{0:T(1024)} %param.12) | copy-start | bytes 98308
  629.9 5.8 copy-start.1
Sparse Core Ops, SparseCore 0:
  9.4 38.1 all-gather.11
  52.1 139.4 all-gather.9
  196.0 129.5 all-gather.7
  329.9 196.1 all-gather.5
  530.3 99.6 all-gather.13
